TPU v7x, 32 devices: a whole 2x2x4 slice. The times are simulated.
32 devices in a mesh: rep: 2 (over x), walk: 16 (over z, y, core).
Axes of the slice: x: 2, y: 2, z: 4, core: 2. Of those that a mesh axis runs over, the one named last changes fastest.
Arguments:
- greens: bfloat16 [32, 64, 384], P(('rep', 'walk')), parts along dimension 0, may hold values from -6 to 6
- source: int32 [64], P(('rep', 'walk')), parts along dimension 0, may hold values from 0 to 15, as said below
- counts: int32 [32], P('rep'), parts along dimension 0, may hold values from 1 to 2, as said below
- cholesky: bfloat16 [512, 64, 384], P('walk'), may hold values from -0.0390625 to 0.0390625
Outputs:
- relocated: bfloat16 [64, 64, 384], P(('rep', 'walk')), parts along dimension 0
- exchange_energy: float32 [64], P(('rep', 'walk')), parts along dimension 0
- force_bias: float32 [64, 512], P(('rep', 'walk')), parts along dimension 0
There are 2 independent parts, one for each index of `rep`. A program takes and returns all parts, laid end to end along the dimension named above; an argument that names none is the same for every part. Nothing has to cross between parts.
Inputs may be any that keep to these rules, and one draw needn't show every extreme that they name: `source`: slot s belongs to walk device s div 2. Its walker comes from that device or one of the two devices beside it along the closed loop of walk devices. Slots beyond a device's count also name some walker. Slots 0 to counts[d] - 1 of device d are live.
All inputs are finite; a program needn't handle non-finite values.
Results may differ from a plain program's by a relative error of at most 0.001.
Values may be sent and summed in bfloat16 or wider, within the bound.
A program may use at most 64 MiB of HBM per device.

v0:
```python
import jax
import jax.numpy as jnp
from jax import lax
from jax.sharding import PartitionSpec as P


def padded(block, sides, width):
    for axis, dim in sides:
        count = lax.axis_size(axis)
        forward = [(i, i + 1) for i in range(count - 1)]
        forward.append((count - 1, 0))
        backward = [(target, source) for source, target in forward]
        low = lax.ppermute(
            lax.slice_in_dim(block, block.shape[dim] - width, None, axis=dim), axis, forward
        )
        high = lax.ppermute(lax.slice_in_dim(block, 0, width, axis=dim), axis, backward)
        block = jnp.concatenate([low, block, high], axis=dim)
    return block


def body(greens, source, counts, cholesky):
    walkers = lax.axis_size("walk")
    my_index = lax.axis_index("walk")
    old_slots = greens.shape[0]
    new_slots = source.shape[0]
    chol_dev = cholesky.shape[0]
    occupied = cholesky.shape[1]
    orbitals = cholesky.shape[2]
    nchol = chol_dev * walkers
    nearby = padded(greens, (("walk", 0),), old_slots)
    src_dev = source // old_slots
    relative = (src_dev - my_index + 1) % walkers
    chosen = relative * old_slots + source % old_slots
    my_count = lax.dynamic_index_in_dim(counts, my_index, 0, keepdims=False)
    is_live = jnp.arange(new_slots) < my_count
    relocated = jnp.where(
        is_live[:, None, None], jnp.take(nearby, chosen, axis=0), jnp.zeros((), jnp.bfloat16)
    )
    chol_rows = cholesky.reshape(chol_dev, occupied * orbitals)
    batch_dims = (((2,), (2,)), ((0,), (0,)))

    def group_energy(group_in):
        members = group_in.shape[0]
        spread = jnp.broadcast_to(
            group_in[:, None], (members, chol_dev, occupied, orbitals)
        ).reshape(members * chol_dev, occupied, orbitals)
        stacked = jnp.broadcast_to(cholesky[None], (members, chol_dev, occupied, orbitals)).reshape(
            members * chol_dev, occupied, orbitals
        )
        forward = lax.dot_general(stacked, spread, batch_dims, preferred_element_type=jnp.float32)
        mirrored = lax.dot_general(spread, stacked, batch_dims, preferred_element_type=jnp.float32)
        return -(0.5 / nchol) * jnp.sum((forward * mirrored).reshape(members, -1), axis=1)

    block_in = lax.all_gather(greens, "walk", axis=0, tiled=True)
    total_rows = block_in.shape[0]
    group = 1
    for candidate in range(1, 5):
        if total_rows % candidate == 0:
            group = candidate
    grouped = block_in.reshape(total_rows // group, group, occupied, orbitals)
    energies = lax.map(group_energy, grouped).reshape(total_rows)
    biases = lax.dot_general(
        block_in.reshape(block_in.shape[0], occupied * orbitals),
        chol_rows,
        (((1,), (1,)), ((), ())),
        preferred_element_type=jnp.float32,
    )
    bias_mine, energy_cols = (
        lax.all_to_all(biases, "walk", split_axis=0, concat_axis=1, tiled=True),
        lax.all_to_all(energies[:, None], "walk", split_axis=0, concat_axis=1, tiled=True),
    )
    energy_mine = jnp.sum(energy_cols, axis=1)
    bias_near, energy_near = (
        padded(bias_mine, (("walk", 0),), old_slots),
        padded(energy_mine, (("walk", 0),), old_slots),
    )
    bias_rows = jnp.take(bias_near, chosen, axis=0)
    energy_slot = jnp.take(energy_near, chosen, axis=0)
    exchange_energy = jnp.where(is_live, energy_slot, 0.0)
    force_bias = jnp.where(is_live[:, None], bias_rows, 0.0)
    return (relocated, exchange_energy, force_bias)


def solution(mesh):
    return jax.shard_map(
        body,
        mesh=mesh,
        in_specs=(
            P(("rep", "walk"), None, None),
            P(("rep", "walk")),
            P("rep"),
            P("walk", None, None),
        ),
        out_specs=(P(("rep", "walk"), None, None), P(("rep", "walk")), P(("rep", "walk"), None)),
        check_vma=False,
    )
```

profile of v0, /device:TPU:0, one launch (start us, length us, event | category | flops | bytes accessed | tf_op | source)
XLA Modules:
  0.0 130.4 jit_solution(3880565610310121807)
XLA Ops:
  1.1 5.1 %collective-permute-start.1 = (bf16[1,64,384]{2,1,0:T(8,128)(2,1)}, bf16[1,64,384]{2,1,0:T(8,128)(2,1)S(1)}, u32[]{:S(2)}, u32[]{:S(2)}) collective-permute-start(bf16[1,64,384]{2,1,0:T(8,128)(2,1)} %param.6), channel_id=1, source_target_pairs={{1,0},{2,1},{3,2},{4,3},{5,4},{6,5},{7,6},{8,7},{9,8},{10,9},{11,1... | collective-permute-start | bytes 147464 | tf_op jit(solution)/shard_map/ppermute | solution.py:16
  6.2 21.7 %all_gather.3 = bf16[16,64,384]{2,1,0:T(8,128)(2,1)S(1)} all-gather(bf16[1,64,384]{2,1,0:T(8,128)(2,1)} %param.6), channel_id=1, replica_groups=mesh['rep'=2,'walk'=16] {'walk'}, dimensions={0}, use_global_device_ids=true | all-gather | bytes 835584 | tf_op jit(solution)/shard_map/all_gather | solution.py:54
  27.9 68.6 %while.10 = (s32[]{:T(128)}, f32[4,4]{1,0:T(4,128)S(1)}, bf16[4,4,64,384]{3,2,1,0:T(8,128)(2,1)S(1)}, bf16[32,64,384]{2,1,0:T(8,128)(2,1)}, s32[]{:T(128)}, /*index=5*/f32[]{:T(128)}, s32[]{:T(128)}) while((s32[]{:T(128)}, f32[4,4]{1,0:T(4,128)S(1)}, bf16[4,4,64,384]{3,2,1,0:T(8,128)(2,1)S(1)}, bf16[32,64,384]{2,1,0:T(8,128)(2,1)}, s32[]{:T(128)}, ...), condition=%wide.region_3.4_spmd, body=%wide.region_0.3_spmd.sunk | while | flops 403701760 | bytes 44107972 | solution.py:61
  28.0 1.0 broadcast_in_dim.91
  29.4 1.0 broadcast_in_dim.92
  30.4 4.3 %fusion.14 = f32[128,64,64]{2,1,0:T(8,128)} fusion(bf16[128,64,384]{2,1,0:T(8,128)(2,1)S(1)} %bitcast.33, bf16[128,64,384]{2,1,0:T(8,128)(2,1)S(1)} %bitcast.34), kind=kOutput, calls=%fused_computation.24.clone.1 | convolution fusion | flops 402653184 | bytes 14680064 | tf_op jit(solution)/shard_map/while/body/eval_jaxpr/dot_general | solution.py:50
  34.7 5.7 %copy.25 = f32[128,64,64]{1,2,0:T(8,128)} copy(f32[128,64,64]{2,1,0:T(8,128)} %fusion.14) | data formatting | bytes 4194304 | tf_op jit(solution)/shard_map/while/body/eval_jaxpr/dot_general | solution.py:50
  40.3 4.5 %fusion.15 = f32[128]{0:T(128)S(1)} fusion(f32[128,64,64]{2,1,0:T(8,128)} %fusion.14, f32[128,64,64]{1,2,0:T(8,128)} %copy.25), kind=kLoop, calls=%fused_computation.4.clone.1 | loop fusion | flops 1048448 | bytes 4194816 | tf_op jit(solution)/shard_map/while/body/eval_jaxpr/reduce_sum | solution.py:52
  45.1 1.0 broadcast_in_dim.91
  46.5 1.0 broadcast_in_dim.92
  47.6 4.3 %fusion.14 = f32[128,64,64]{2,1,0:T(8,128)} fusion(bf16[128,64,384]{2,1,0:T(8,128)(2,1)S(1)} %bitcast.33, bf16[128,64,384]{2,1,0:T(8,128)(2,1)S(1)} %bitcast.34), kind=kOutput, calls=%fused_computation.24.clone.1 | convolution fusion | flops 402653184 | bytes 14680064 | tf_op jit(solution)/shard_map/while/body/eval_jaxpr/dot_general | solution.py:50
  51.8 5.7 %copy.25 = f32[128,64,64]{1,2,0:T(8,128)} copy(f32[128,64,64]{2,1,0:T(8,128)} %fusion.14) | data formatting | bytes 4194304 | tf_op jit(solution)/shard_map/while/body/eval_jaxpr/dot_general | solution.py:50
  57.5 4.5 %fusion.15 = f32[128]{0:T(128)S(1)} fusion(f32[128,64,64]{2,1,0:T(8,128)} %fusion.14, f32[128,64,64]{1,2,0:T(8,128)} %copy.25), kind=kLoop, calls=%fused_computation.4.clone.1 | loop fusion | flops 1048448 | bytes 4194816 | tf_op jit(solution)/shard_map/while/body/eval_jaxpr/reduce_sum | solution.py:52
  62.3 1.0 broadcast_in_dim.91
  63.7 1.0 broadcast_in_dim.92
  64.7 4.3 %fusion.14 = f32[128,64,64]{2,1,0:T(8,128)} fusion(bf16[128,64,384]{2,1,0:T(8,128)(2,1)S(1)} %bitcast.33, bf16[128,64,384]{2,1,0:T(8,128)(2,1)S(1)} %bitcast.34), kind=kOutput, calls=%fused_computation.24.clone.1 | convolution fusion | flops 402653184 | bytes 14680064 | tf_op jit(solution)/shard_map/while/body/eval_jaxpr/dot_general | solution.py:50
  69.0 5.7 %copy.25 = f32[128,64,64]{1,2,0:T(8,128)} copy(f32[128,64,64]{2,1,0:T(8,128)} %fusion.14) | data formatting | bytes 4194304 | tf_op jit(solution)/shard_map/while/body/eval_jaxpr/dot_general | solution.py:50
  74.6 4.5 %fusion.15 = f32[128]{0:T(128)S(1)} fusion(f32[128,64,64]{2,1,0:T(8,128)} %fusion.14, f32[128,64,64]{1,2,0:T(8,128)} %copy.25), kind=kLoop, calls=%fused_computation.4.clone.1 | loop fusion | flops 1048448 | bytes 4194816 | tf_op jit(solution)/shard_map/while/body/eval_jaxpr/reduce_sum | solution.py:52
  79.4 1.0 broadcast_in_dim.91
  80.8 1.0 broadcast_in_dim.92
  81.8 4.3 %fusion.14 = f32[128,64,64]{2,1,0:T(8,128)} fusion(bf16[128,64,384]{2,1,0:T(8,128)(2,1)S(1)} %bitcast.33, bf16[128,64,384]{2,1,0:T(8,128)(2,1)S(1)} %bitcast.34), kind=kOutput, calls=%fused_computation.24.clone.1 | convolution fusion | flops 402653184 | bytes 14680064 | tf_op jit(solution)/shard_map/while/body/eval_jaxpr/dot_general | solution.py:50
  86.1 5.7 %copy.25 = f32[128,64,64]{1,2,0:T(8,128)} copy(f32[128,64,64]{2,1,0:T(8,128)} %fusion.14) | data formatting | bytes 4194304 | tf_op jit(solution)/shard_map/while/body/eval_jaxpr/dot_general | solution.py:50
  91.8 4.5 %fusion.15 = f32[128]{0:T(128)S(1)} fusion(f32[128,64,64]{2,1,0:T(8,128)} %fusion.14, f32[128,64,64]{1,2,0:T(8,128)} %copy.25), kind=kLoop, calls=%fused_computation.4.clone.1 | loop fusion | flops 1048448 | bytes 4194816 | tf_op jit(solution)/shard_map/while/body/eval_jaxpr/reduce_sum | solution.py:52
  97.2 3.5 %all-to-all-start = ((f32[16,1,1]{2,1,0:T(1,128)}), f32[16,1,1]{2,1,0:T(1,128)S(1)}, u32[]{:S(2)}, u32[]{:S(2)}) async-start(f32[16,1,1]{2,1,0:T(1,128)} %all_to_all.27), calls=%async_computation | async-start | bytes 16384 | tf_op jit(solution)/shard_map/all_to_all | solution.py:70
  100.7 3.7 %fusion.1 = f32[16,32,1]{1,0,2:T(8,128)} fusion(bf16[32,64,384]{2,1,0:T(8,128)(2,1)} %get-tuple-element.91, bf16[16,64,384]{2,1,0:T(8,128)(2,1)S(1)} %bitcast.36), kind=kOutput, calls=%fused_computation.7 | convolution fusion | flops 25165824 | bytes 2361344 | tf_op jit(solution)/shard_map/dot_general | solution.py:62
  105.7 1.3 all-to-all-done
  107.0 4.7 %all-to-all-start.1 = ((f32[16,1,32]{2,1,0:T(1,128)}), f32[16,1,32]{2,1,0:T(1,128)S(1)}, u32[]{:S(2)}, u32[]{:S(2)}) async-start(f32[16,1,32]{2,1,0:T(1,128)} %bitcast.10), calls=%async_computation.1 | async-start | bytes 16384 | tf_op jit(solution)/shard_map/all_to_all | solution.py:69
  112.7 4.0 %collective-permute-start.3 = (f32[1]{0:T(128)}, f32[1]{0:T(128)}, u32[]{:S(2)}, u32[]{:S(2)}) collective-permute-start(f32[1]{0:T(128)} %bitcast.7), channel_id=1, source_target_pairs={{1,0},{2,1},{3,2},{4,3},{5,4},{6,5},{7,6},{8,7},{9,8},{10,9},{11,1... | collective-permute-start | bytes 20 | tf_op jit(solution)/shard_map/ppermute | solution.py:16
  116.8 1.3 %collective-permute-done.2 = f32[1]{0:T(128)} collective-permute-done((f32[1]{0:T(128)}, f32[1]{0:T(128)}, u32[]{:S(2)}, u32[]{:S(2)}) %collective-permute-start.2) | collective-permute-done | bytes 36 | tf_op jit(solution)/shard_map/ppermute | solution.py:13
  118.2 2.0 %pad_maximum_fusion.2 = f32[3]{0:T(128)S(1)} fusion(f32[1]{0:T(128)} %collective-permute-done.3, f32[1]{0:T(128)} %bitcast.7, f32[1]{0:T(128)} %collective-permute-done.2), kind=kLoop, calls=%fused_computation.21 | loop fusion | flops 6 | bytes 24 | tf_op jit(solution)/shard_map/concatenate | solution.py:17
  122.1 4.4 %collective-permute-start.5 = (f32[1,512]{1,0:T(1,128)S(1)}, f32[1,512]{1,0:T(1,128)S(1)}, u32[]{:S(2)}, u32[]{:S(2)}) collective-permute-start(f32[1,512]{1,0:T(1,128)S(1)} %all_to_all.26), channel_id=1, source_target_pairs={{1,0},{2,1},{3,2},{4,3},{5,4},{6,5},{7,6},{8,7},{9,8},{10,9},{11,1... | collective-permute-start | bytes 6152 | tf_op jit(solution)/shard_map/ppermute | solution.py:16
  126.5 1.2 select_select_fusion.2
  (59 shorter events, 10.7 us)
Async XLA Ops:
  0.6 128.4 %collective-permute-start = (bf16[1,64,384]{2,1,0:T(8,128)(2,1)}, bf16[1,64,384]{2,1,0:T(8,128)(2,1)S(1)}, u32[]{:S(2)}, u32[]{:S(2)}) collective-permute-start(bf16[1,64,384]{2,1,0:T(8,128)(2,1)} %param.6), channel_id=1, source_target_pairs={{0,1},{1,2},{2,3},{3,4},{4,5},{5,6},{6,7},{7,8},{8,9},{9,10},{10,1... | collective-permute-start | bytes 147464 | tf_op jit(solution)/shard_map/ppermute | solution.py:13
  1.1 127.9 %collective-permute-start.1 = (bf16[1,64,384]{2,1,0:T(8,128)(2,1)}, bf16[1,64,384]{2,1,0:T(8,128)(2,1)S(1)}, u32[]{:S(2)}, u32[]{:S(2)}) collective-permute-start(bf16[1,64,384]{2,1,0:T(8,128)(2,1)} %param.6), channel_id=1, source_target_pairs={{1,0},{2,1},{3,2},{4,3},{5,4},{6,5},{7,6},{8,7},{9,8},{10,9},{11,1... | collective-permute-start | bytes 147464 | tf_op jit(solution)/shard_map/ppermute | solution.py:16
  27.9 76.5 %copy-start.3 = (s32[16]{0:T(128)S(1)}, s32[16]{0:T(128)}, u32[]{:S(2)}) copy-start(s32[16]{0:T(128)} %param.8) | copy-start | bytes 196
  27.9 77.1 %copy-start.2 = (s32[2]{0:T(128)S(1)}, s32[2]{0:T(128)}, u32[]{:S(2)}) copy-start(s32[2]{0:T(128)} %param.7) | copy-start | bytes 28
  27.9 101.2 %copy-start.1 = (bf16[1,64,384]{2,1,0:T(8,128)(2,1)S(1)}, bf16[1,64,384]{2,1,0:T(8,128)(2,1)}, u32[]{:S(2)}) copy-start(bf16[1,64,384]{2,1,0:T(8,128)(2,1)} %param.6) | copy-start | bytes 147460
  27.9 1.4 %copy-start = (bf16[32,64,384]{2,1,0:T(8,128)(2,1)S(1)}, bf16[32,64,384]{2,1,0:T(8,128)(2,1)}, u32[]{:S(2)}) copy-start(bf16[32,64,384]{2,1,0:T(8,128)(2,1)} %get-tuple-element.87) | copy-start | bytes 4718596 | tf_op jit(solution)/shard_map/while
  45.1 1.4 %copy-start = (bf16[32,64,384]{2,1,0:T(8,128)(2,1)S(1)}, bf16[32,64,384]{2,1,0:T(8,128)(2,1)}, u32[]{:S(2)}) copy-start(bf16[32,64,384]{2,1,0:T(8,128)(2,1)} %get-tuple-element.87) | copy-start | bytes 4718596 | tf_op jit(solution)/shard_map/while
  62.2 1.4 %copy-start = (bf16[32,64,384]{2,1,0:T(8,128)(2,1)S(1)}, bf16[32,64,384]{2,1,0:T(8,128)(2,1)}, u32[]{:S(2)}) copy-start(bf16[32,64,384]{2,1,0:T(8,128)(2,1)} %get-tuple-element.87) | copy-start | bytes 4718596 | tf_op jit(solution)/shard_map/while
  79.4 1.4 %copy-start = (bf16[32,64,384]{2,1,0:T(8,128)(2,1)S(1)}, bf16[32,64,384]{2,1,0:T(8,128)(2,1)}, u32[]{:S(2)}) copy-start(bf16[32,64,384]{2,1,0:T(8,128)(2,1)} %get-tuple-element.87) | copy-start | bytes 4718596 | tf_op jit(solution)/shard_map/while
  97.2 9.8 %all-to-all-start = ((f32[16,1,1]{2,1,0:T(1,128)}), f32[16,1,1]{2,1,0:T(1,128)S(1)}, u32[]{:S(2)}, u32[]{:S(2)}) async-start(f32[16,1,1]{2,1,0:T(1,128)} %all_to_all.27), calls=%async_computation | async-start | bytes 16384 | tf_op jit(solution)/shard_map/all_to_all | solution.py:70
  107.0 13.8 %all-to-all-start.1 = ((f32[16,1,32]{2,1,0:T(1,128)}), f32[16,1,32]{2,1,0:T(1,128)S(1)}, u32[]{:S(2)}, u32[]{:S(2)}) async-start(f32[16,1,32]{2,1,0:T(1,128)} %bitcast.10), calls=%async_computation.1 | async-start | bytes 16384 | tf_op jit(solution)/shard_map/all_to_all | solution.py:69
  112.3 5.7 %collective-permute-start.2 = (f32[1]{0:T(128)}, f32[1]{0:T(128)}, u32[]{:S(2)}, u32[]{:S(2)}) collective-permute-start(f32[1]{0:T(128)} %bitcast.7), channel_id=1, source_target_pairs={{0,1},{1,2},{2,3},{3,4},{4,5},{5,6},{6,7},{7,8},{8,9},{9,10},{10,1... | collective-permute-start | bytes 20 | tf_op jit(solution)/shard_map/ppermute | solution.py:13
  112.7 5.5 %collective-permute-start.3 = (f32[1]{0:T(128)}, f32[1]{0:T(128)}, u32[]{:S(2)}, u32[]{:S(2)}) collective-permute-start(f32[1]{0:T(128)} %bitcast.7), channel_id=1, source_target_pairs={{1,0},{2,1},{3,2},{4,3},{5,4},{6,5},{7,6},{8,7},{9,8},{10,9},{11,1... | collective-permute-start | bytes 20 | tf_op jit(solution)/shard_map/ppermute | solution.py:16
  122.1 5.7 %collective-permute-start.4 = (f32[1,512]{1,0:T(1,128)S(1)}, f32[1,512]{1,0:T(1,128)S(1)}, u32[]{:S(2)}, u32[]{:S(2)}) collective-permute-start(f32[1,512]{1,0:T(1,128)S(1)} %all_to_all.26), channel_id=1, source_target_pairs={{0,1},{1,2},{2,3},{3,4},{4,5},{5,6},{6,7},{7,8},{8,9},{9,10},{10,1... | collective-permute-start | bytes 6152 | tf_op jit(solution)/shard_map/ppermute | solution.py:13
  122.1 5.7 %collective-permute-start.5 = (f32[1,512]{1,0:T(1,128)S(1)}, f32[1,512]{1,0:T(1,128)S(1)}, u32[]{:S(2)}, u32[]{:S(2)}) collective-permute-start(f32[1,512]{1,0:T(1,128)S(1)} %all_to_all.26), channel_id=1, source_target_pairs={{1,0},{2,1},{3,2},{4,3},{5,4},{6,5},{7,6},{8,7},{9,8},{10,9},{11,1... | collective-permute-start | bytes 6152 | tf_op jit(solution)/shard_map/ppermute | solution.py:16
where the time goes:
time: 131 us; the launch traced here: 130 us
  local copies, waits for them, and re-layouts  36.5 us (28%)
  other arithmetic  25 us (19%)
  starting transfers between devices  22.6 us (17%)
  blocking collectives  21.7 us (17%)
  matrix products  20.8 us (16%)
  waiting for transfers between devices  2.86 us (2%)
    dot_general x4, local copies, waits for them, and re-layouts, group_energy(): lax.dot_general(stacked, spread, batch_dims, preferred_element_type=jnp.f...  22.6 us
    all_gather x1, blocking collectives, body(): block_in = lax.all_gather(greens, 'walk', axis=0, tiled=True)  21.7 us
    reduce_sum x8, other arithmetic, group_energy(): jnp.sum((forward * mirrored).reshape(members, -1), axis=1)  18.5 us
    dot_general x4, matrix products, group_energy(): lax.dot_general(stacked, spread, batch_dims, preferred_element_type=jnp.f...  17.1 us
    ppermute x3, starting transfers between devices, padded(): lax.ppermute(lax.slice_in_dim(block, 0, width, axis=dim), axis, backward)  13.5 us
    all_to_all x1, starting transfers between devices, body(): lax.all_to_all(biases, 'walk', split_axis=0, concat_axis=1, tiled=True)  4.71 us
    broadcast_in_dim x8, local copies, waits for them, and re-layouts, group_energy(): jnp.broadcast_to(group_in[:, None], (members, chol_dev, occupied, orbitals))  4.26 us
    broadcast_in_dim x4, local copies, waits for them, and re-layouts, group_energy(): jnp.broadcast_to(cholesky[None], (members, chol_dev, occupied, orbitals))  4.15 us
  transfers between devices with their start and end apart: 8, of which 4 were waited for; matrix products, arithmetic and copies ran while one was open for 61% of the time, Pallas kernels for 0%

commit v1 on v0

v1 whole, which is shorter than its diff:
```python
import functools

import jax
import jax.numpy as jnp
from jax import lax
from jax.experimental import pallas as pl
from jax.experimental.pallas import tpu as pltpu
from jax.sharding import PartitionSpec as P

MESH = pl.DeviceIdType.MESH
NEAR = 3
TILE = 4
STEP = 8


def flip(index, mask):
    bit = 1
    while bit <= mask:
        if mask & bit:
            index = index + bit - 2 * bit * ((index // bit) % 2)
        bit *= 2
    return index


def kernel(
    n, nocc, chol_dev, nchol,
    source_ref, counts_ref, greens_ref, chol_ref,
    reloc_ref, energy_ref, bias_ref,
    walkers, chol, diag, message, inbox, reloc,
    local_sem, line_send, pair_send, core_send, walker_recv, mail_send, mail_recv,
):
    me = lax.axis_index("walk")
    depth = n // 4
    core = me % 2
    side = (me // 2) % 2
    z = me // 4

    def slot_of(zz, ss, cc):
        return (cc * 2 + ss) * depth + zz

    def device_of(zz, ss, cc):
        return (zz * 2 + ss) * 2 + cc

    mine = slot_of(z, side, core)
    load_own = pltpu.make_async_copy(greens_ref, walkers.at[mine], local_sem.at[0])
    load_own.start()
    load_chol = pltpu.make_async_copy(chol_ref, chol, local_sem.at[1])
    load_chol.start()

    barrier = pltpu.get_barrier_semaphore()
    for k in range(1, n):
        pl.semaphore_signal(
            barrier, inc=1, device_id={"walk": (me + k) % n}, device_id_type=MESH
        )
    diag[...] = jnp.zeros_like(diag)
    load_own.wait()
    pl.semaphore_wait(barrier, n - 1)

    def send(slot, sem, target):
        copy = pltpu.make_async_remote_copy(
            src_ref=walkers.at[slot],
            dst_ref=walkers.at[slot],
            send_sem=sem,
            recv_sem=walker_recv.at[slot],
            device_id={"walk": target},
            device_id_type=MESH,
        )
        copy.start()
        return copy

    def arrived(slot):
        pltpu.make_async_remote_copy(
            src_ref=walkers.at[slot],
            dst_ref=walkers.at[slot],
            send_sem=local_sem.at[0],
            recv_sem=walker_recv.at[slot],
            device_id={"walk": me},
            device_id_type=MESH,
        ).wait_recv()

    other = 1 - side
    sibling = device_of(z, side, 1 - core)
    partner = device_of(z, other, core)
    sent = [send(mine, pair_send.at[0], partner)]
    for k in range(1, depth):
        sent.append(send(mine, line_send.at[k], device_of(flip(z, k), side, core)))
    sent.append(send(mine, core_send.at[0], sibling))
    for k in range(1, depth):
        slot = slot_of(flip(z, k), side, core)
        arrived(slot)
        sent.append(send(slot, pair_send.at[k], partner))
        sent.append(send(slot, core_send.at[k], sibling))

    lane8 = lax.broadcasted_iota(jnp.int32, (8, 128), 1)
    row8 = lax.broadcasted_iota(jnp.int32, (8, 128), 0)
    low = lax.broadcasted_iota(jnp.int32, (nocc, 128), 1) < nocc
    on_diag = (lane8 % 8) == row8
    bands = [(lane8 % nocc) // 8 == r for r in range(nocc // 8)]
    shift = (me % 4) * chol_dev
    energy_row = pl.multiple_of((shift + chol_dev) % 128, 8)

    def compute(first):
        group = walkers[pl.ds(first, TILE)].reshape(TILE * nocc, -1)
        nt = (((1,), (1,)), ((), ()))

        def chunk(c, sums):
            rows = STEP * nocc
            part = chol[pl.ds(pl.multiple_of(c * rows, rows), rows), :]
            forward = lax.dot_general(part, group, nt, preferred_element_type=jnp.float32)
            mirror = lax.dot_general(group, part, nt, preferred_element_type=jnp.float32)
            out = []
            for wp in range(TILE // 2):
                lanes = slice(wp * 128, wp * 128 + 128)
                total = sums[wp]
                for gp in range(STEP // 2):
                    cols = slice(gp * 128, gp * 128 + 128)
                    f0 = forward[gp * 128 : gp * 128 + nocc, lanes]
                    f1 = forward[gp * 128 + nocc : gp * 128 + 128, lanes]
                    m0 = mirror[wp * 128 : wp * 128 + nocc, cols]
                    m1 = mirror[wp * 128 + nocc : wp * 128 + 128, cols]
                    turned = pltpu.roll(jnp.where(low, m1, m0), nocc, 1)
                    product = jnp.where(low, f0, f1) * jnp.where(low, m0, m1)
                    product = product + jnp.where(low, f1, f0) * turned
                    total = total + jnp.sum(product.reshape(nocc // 8, 8, 128), axis=0)
                out.append(total)
                block = jnp.zeros((8, 128), jnp.float32)
                for g in range(STEP):
                    picked = forward[g * nocc : g * nocc + 8, lanes]
                    for r in range(1, nocc // 8):
                        at = g * nocc + r * 8
                        picked = jnp.where(bands[r], forward[at : at + 8, lanes], picked)
                    line = jnp.sum(jnp.where(on_diag, picked, 0.0), axis=0, keepdims=True)
                    block = jnp.where(row8 == g, line, block)
                at = pl.multiple_of(shift + c * STEP, 8)
                diag[pl.ds(at, STEP), pl.ds(first * nocc + wp * 128, 128)] = block
            return tuple(out)

        zero = jnp.zeros((8, 128), jnp.float32)
        sums = lax.fori_loop(0, chol_dev // STEP, chunk, (zero,) * (TILE // 2))
        for wp in range(TILE // 2):
            at = pl.multiple_of(first * nocc + wp * 128, 128)
            diag[pl.ds(energy_row, 8), pl.ds(at, 128)] = sums[wp]

    def compute_group(ss, cc):
        for part in range(depth // TILE):
            compute(pl.multiple_of(slot_of(part * TILE, ss, cc), TILE))

    load_chol.wait()
    compute_group(side, core)
    for k in range(depth):
        slot = slot_of(flip(z, k), other, core)
        arrived(slot)
        sent.append(send(slot, core_send.at[depth + k], sibling))
    compute_group(other, core)
    for ss in (side, other):
        for k in range(depth):
            arrived(slot_of(flip(z, k), ss, 1 - core))
        compute_group(ss, 1 - core)

    table = jnp.sum(diag[...].T.reshape(n, nocc, 128), axis=1)
    for w in range(n):
        slot = slot_of(w // 4, (w // 2) % 2, w % 2)
        message[w + 1, :, :] = table[slot : slot + 1, :]
        if w == 0:
            message[n + 1, :, :] = table[slot : slot + 1, :]
        if w == n - 1:
            message[0, :, :] = table[slot : slot + 1, :]
    mail = []
    for k in range(1, n):
        target = (me + k) % n
        copy = pltpu.make_async_remote_copy(
            src_ref=message.at[pl.ds(target, NEAR)],
            dst_ref=inbox.at[me],
            send_sem=mail_send.at[k],
            recv_sem=mail_recv.at[me],
            device_id={"walk": target},
            device_id_type=MESH,
        )
        copy.start()
        mail.append(copy)
    inbox[pl.ds(me, 1)] = message[pl.ds(me, NEAR)][None]

    my_count = counts_ref[me]
    slots = reloc.shape[0]
    chosen = []
    for s in range(slots):
        w = jnp.clip(source_ref[s], 0, n - 1)
        slot = slot_of(w // 4, (w // 2) % 2, w % 2)
        live = s < my_count
        value = walkers[slot]
        reloc[s] = jnp.where(live, value, jnp.zeros_like(value))
        near = jnp.minimum(lax.rem(w - me + 1 + n, n), NEAR - 1)
        chosen.append((near, live))
    store = pltpu.make_async_copy(reloc, reloc_ref, local_sem.at[2])
    store.start()

    for k in range(1, n):
        origin = (me + k) % n
        pltpu.make_async_remote_copy(
            src_ref=message.at[pl.ds(0, NEAR)],
            dst_ref=inbox.at[origin],
            send_sem=local_sem.at[0],
            recv_sem=mail_recv.at[origin],
            device_id={"walk": me},
            device_id_type=MESH,
        ).wait_recv()

    lane1 = lax.broadcasted_iota(jnp.int32, (1, 128), 1)
    per = 128 // chol_dev
    for s, (near, live) in enumerate(chosen):
        energy = jnp.zeros((1, 128), jnp.float32)
        for b in range(n // per):
            row = jnp.zeros((1, 128), jnp.float32)
            for q in range(per):
                got = inbox[b * per + q, near]
                row = jnp.where(lane1 // chol_dev == q, got, row)
                rest = (lane1 + (128 - (q + 1) * chol_dev)) % 128
                energy = energy + jnp.where(rest < 8, got, 0.0)
            bias_ref[s : s + 1, b * 128 : b * 128 + 128] = jnp.where(live, row, 0.0)
        energy_ref[s] = jnp.where(live, jnp.sum(energy) * (-0.5 / nchol), 0.0)

    for copy in sent + mail:
        copy.wait_send()
    store.wait()


def body(greens, source, counts, cholesky):
    n = lax.axis_size("walk")
    chol_dev, nocc, orbitals = cholesky.shape
    slots = source.shape[0]
    nchol = chol_dev * n
    assert greens.shape[0] == 1 and nocc == 64 and chol_dev == 32
    depth = n // 4
    return pl.pallas_call(
        functools.partial(kernel, n, nocc, chol_dev, nchol),
        out_shape=(
            jax.ShapeDtypeStruct((slots, nocc, orbitals), jnp.bfloat16),
            jax.ShapeDtypeStruct((slots,), jnp.float32),
            jax.ShapeDtypeStruct((slots, nchol), jnp.float32),
        ),
        in_specs=[
            pl.BlockSpec(memory_space=pltpu.SMEM),
            pl.BlockSpec(memory_space=pltpu.SMEM),
            pl.BlockSpec(memory_space=pl.ANY),
            pl.BlockSpec(memory_space=pl.ANY),
        ],
        out_specs=(
            pl.BlockSpec(memory_space=pl.ANY),
            pl.BlockSpec(memory_space=pltpu.SMEM),
            pl.BlockSpec(memory_space=pltpu.VMEM),
        ),
        scratch_shapes=[
            pltpu.VMEM((n, nocc, orbitals), jnp.bfloat16),
            pltpu.VMEM((chol_dev * nocc, orbitals), jnp.bfloat16),
            pltpu.VMEM((128, n * nocc), jnp.float32),
            pltpu.VMEM((n + 2, 1, 128), jnp.float32),
            pltpu.VMEM((n, NEAR, 1, 128), jnp.float32),
            pltpu.VMEM((slots, nocc, orbitals), jnp.bfloat16),
            pltpu.SemaphoreType.DMA((3,)),
            pltpu.SemaphoreType.DMA((depth,)),
            pltpu.SemaphoreType.DMA((depth,)),
            pltpu.SemaphoreType.DMA((2 * depth,)),
            pltpu.SemaphoreType.DMA((n,)),
            pltpu.SemaphoreType.DMA((n,)),
            pltpu.SemaphoreType.DMA((n,)),
        ],
        compiler_params=pltpu.CompilerParams(collective_id=0, has_side_effects=True),
    )(source, counts, greens.reshape(nocc, orbitals), cholesky.reshape(chol_dev * nocc, orbitals))


def solution(mesh):
    return jax.shard_map(
        body,
        mesh=mesh,
        in_specs=(
            P(("rep", "walk"), None, None),
            P(("rep", "walk")),
            P("rep"),
            P("walk", None, None),
        ),
        out_specs=(P(("rep", "walk"), None, None), P(("rep", "walk")), P(("rep", "walk"), None)),
        check_vma=False,
    )
```

time: 131 us -> 32.8 us (0.25)
  local copies, waits for them, and re-layouts: 36.5 us -> 3.92 us
  Pallas kernels: 0 us -> 28 us
  other arithmetic: 25 us -> 0 us
  starting transfers between devices: 22.6 us -> 0 us
  blocking collectives: 21.7 us -> 0 us
  matrix products: 20.8 us -> 0 us
  waiting for transfers between devices: 2.86 us -> 0 us
    pallas_call x0 -> x1, Pallas kernels: none -> 28 us  [body(): pl.pallas_call(functools.partial(kernel, n, nocc, chol_dev, nchol), out_s...]
    dot_general x4 -> x0, local copies, waits for them, and re-layouts: 22.6 us -> none  [group_energy(): lax.dot_general(stacked, spread, batch_dims, preferred_element_type=jnp.f...]
    all_gather x1 -> x0, blocking collectives: 21.7 us -> none  [body(): block_in = lax.all_gather(greens, 'walk', axis=0, tiled=True)]
    dot_general x5 -> x0, matrix products: 20.8 us -> none  [the longest x4 17.1 us: group_energy(): lax.dot_general(stacked, spread, batch_dims, preferred_element_type=jnp.f...]
    reduce_sum x9 -> x0, other arithmetic: 19.1 us -> none  [the longest x8 18.5 us: group_energy(): jnp.sum((forward * mirrored).reshape(members, -1), axis=1)]
    ppermute x6 -> x0, starting transfers between devices: 14.5 us -> none  [the longest x3 13.5 us: padded(): lax.ppermute(lax.slice_in_dim(block, 0, width, axis=dim), axis, backward)]
    broadcast_in_dim x12 -> x0, local copies, waits for them, and re-layouts: 8.41 us -> none  [the longest x8 4.26 us: group_energy(): jnp.broadcast_to(group_in[:, None], (members, chol_dev, occupied, orbitals))]
    all_to_all x2 -> x0, starting transfers between devices: 8.18 us -> none  [the longest x1 4.71 us: body(): lax.all_to_all(biases, 'walk', split_axis=0, concat_axis=1, tiled=True)]
  transfers between devices with their start and end apart: 8 -> 0, of which waited for: 4 -> 0; matrix products, arithmetic and copies ran while one was open for 61% -> 0% of each run, Pallas kernels for 0% -> 0%
where the time goes in v1:
time: 32.8 us; the launch traced here: 32.6 us
  Pallas kernels  28 us (85%)
  local copies, waits for them, and re-layouts  3.92 us (12%)
  between operations  0.64 us (2%)
    pallas_call x1, Pallas kernels, body(): pl.pallas_call(functools.partial(kernel, n, nocc, chol_dev, nchol), out_s...  28 us
    unnamed x3, local copies, waits for them, and re-layouts  3.92 us

profile of v1, /device:TPU:0, one launch (start us, length us, event | category | flops | bytes accessed | tf_op | source)
XLA Modules:
  0.0 32.6 jit_solution(5484309003438428881)
XLA Ops:
  0.6 28.0 %shard_map.67 = (bf16[2,64,384]{2,1,0:T(8,128)(2,1)}, f32[2]{0:T(128)}, f32[2,512]{1,0:T(2,128)}) custom-call(s32[2]{0:T(128)} %source_ref.1, s32[16]{0:T(128)} %counts_ref.1, bf16[64,384]{1,0:T(8,128)(2,1)} %bitcast.3, bf16[2048,384]{1,0:T(8,128)(2,1)} %bitcast.2), custom_call_target="tpu_custom_call" | custom-call | tf_op jit(solution)/shard_map/pallas_call | solution.py:234
  28.7 1.5 %copy.10 = bf16[2,64,384]{2,1,0:T(8,128)(2,1)} copy(bf16[2,64,384]{2,1,0:T(8,128)(2,1)} %get-tuple-element.6) | data formatting | bytes 196608
  30.2 1.1 %copy.11 = f32[2]{0:T(128)} copy(f32[2]{0:T(128)} %get-tuple-element.7) | data formatting | bytes 16
  31.3 1.3 %copy.12 = f32[2,512]{1,0:T(2,128)} copy(f32[2,512]{1,0:T(2,128)} %get-tuple-element.8) | data formatting | bytes 8192

commit v2 on v1

--- a/solution.py
+++ b/solution.py
@@ -26,7 +26,7 @@
     n, nocc, chol_dev, nchol,
     source_ref, counts_ref, greens_ref, chol_ref,
     reloc_ref, energy_ref, bias_ref,
-    walkers, chol, diag, message, inbox, reloc,
+    walkers, chol, chol_t, group_t, diag, message, inbox, reloc,
     local_sem, line_send, pair_send, core_send, walker_recv, mail_send, mail_recv,
 ):
     me = lax.axis_index("walk")
@@ -35,14 +35,16 @@
     side = (me // 2) % 2
     z = me // 4
 
-    def slot_of(zz, ss, cc):
-        return (cc * 2 + ss) * depth + zz
+    def slot_of(k, s, c):
+        return jnp.where(k == 0, s * 2 + c, 4 + s * 2 * (depth - 1) + (k - 1) * 2 + c)
+
+    def place(k, s, c):
+        return s * 2 + c if k == 0 else 4 + s * 2 * (depth - 1) + (k - 1) * 2 + c
 
     def device_of(zz, ss, cc):
         return (zz * 2 + ss) * 2 + cc
 
-    mine = slot_of(z, side, core)
-    load_own = pltpu.make_async_copy(greens_ref, walkers.at[mine], local_sem.at[0])
+    load_own = pltpu.make_async_copy(greens_ref, walkers.at[0], local_sem.at[0])
     load_own.start()
     load_chol = pltpu.make_async_copy(chol_ref, chol, local_sem.at[1])
     load_chol.start()
@@ -56,19 +58,22 @@
     load_own.wait()
     pl.semaphore_wait(barrier, n - 1)
 
-    def send(slot, sem, target):
+    def send(src, dst, sem, target):
         copy = pltpu.make_async_remote_copy(
-            src_ref=walkers.at[slot],
-            dst_ref=walkers.at[slot],
+            src_ref=walkers.at[src],
+            dst_ref=walkers.at[dst],
             send_sem=sem,
-            recv_sem=walker_recv.at[slot],
+            recv_sem=walker_recv.at[dst],
             device_id={"walk": target},
             device_id_type=MESH,
         )
         copy.start()
-        return copy
-
-    def arrived(slot):
+        sent.append(copy)
+
+    sent = []
+
+    def arrived(k, s, c):
+        slot = place(k, s, c)
         pltpu.make_async_remote_copy(
             src_ref=walkers.at[slot],
             dst_ref=walkers.at[slot],
@@ -81,15 +86,23 @@
     other = 1 - side
     sibling = device_of(z, side, 1 - core)
     partner = device_of(z, other, core)
-    sent = [send(mine, pair_send.at[0], partner)]
+
+    def to_partner(k):
+        send(place(k, 0, 0), place(k, 1, 0), pair_send.at[k], partner)
+
+    def to_sibling(k, s):
+        send(place(k, s, 0), place(k, s, 1), core_send.at[s * depth + k], sibling)
+
+    to_partner(0)
     for k in range(1, depth):
-        sent.append(send(mine, line_send.at[k], device_of(flip(z, k), side, core)))
-    sent.append(send(mine, core_send.at[0], sibling))
-    for k in range(1, depth):
-        slot = slot_of(flip(z, k), side, core)
-        arrived(slot)
-        sent.append(send(slot, pair_send.at[k], partner))
-        sent.append(send(slot, core_send.at[k], sibling))
+        send(0, place(k, 0, 0), line_send.at[k], device_of(flip(z, k), side, core))
+    to_sibling(0, 0)
+    load_chol.wait()
+
+    @pl.loop(0, chol_dev // STEP)
+    def _(c):
+        at = pl.ds(pl.multiple_of(c * (STEP * nocc), STEP * nocc), STEP * nocc)
+        chol_t[:, at] = chol[at, :].T
 
     lane8 = lax.broadcasted_iota(jnp.int32, (8, 128), 1)
     row8 = lax.broadcasted_iota(jnp.int32, (8, 128), 0)
@@ -100,14 +113,15 @@
     energy_row = pl.multiple_of((shift + chol_dev) % 128, 8)
 
     def compute(first):
-        group = walkers[pl.ds(first, TILE)].reshape(TILE * nocc, -1)
-        nt = (((1,), (1,)), ((), ()))
+        group = walkers[first : first + TILE].reshape(TILE * nocc, -1)
+        group_t[...] = group.T
 
         def chunk(c, sums):
             rows = STEP * nocc
             part = chol[pl.ds(pl.multiple_of(c * rows, rows), rows), :]
-            forward = lax.dot_general(part, group, nt, preferred_element_type=jnp.float32)
-            mirror = lax.dot_general(group, part, nt, preferred_element_type=jnp.float32)
+            part_t = chol_t[:, pl.ds(pl.multiple_of(c * rows, rows), rows)]
+            forward = jnp.dot(part, group_t[...], preferred_element_type=jnp.float32)
+            mirror = jnp.dot(group, part_t, preferred_element_type=jnp.float32)
             out = []
             for wp in range(TILE // 2):
                 lanes = slice(wp * 128, wp * 128 + 128)
@@ -136,35 +150,52 @@
             return tuple(out)
 
         zero = jnp.zeros((8, 128), jnp.float32)
-        sums = lax.fori_loop(0, chol_dev // STEP, chunk, (zero,) * (TILE // 2))
+        sums = lax.fori_loop(0, chol_dev // STEP, chunk, (zero,) * (TILE // 2), unroll=True)
         for wp in range(TILE // 2):
-            at = pl.multiple_of(first * nocc + wp * 128, 128)
-            diag[pl.ds(energy_row, 8), pl.ds(at, 128)] = sums[wp]
-
-    def compute_group(ss, cc):
-        for part in range(depth // TILE):
-            compute(pl.multiple_of(slot_of(part * TILE, ss, cc), TILE))
-
-    load_chol.wait()
-    compute_group(side, core)
+            diag[pl.ds(energy_row, 8), pl.ds(first * nocc + wp * 128, 128)] = sums[wp]
+
+    def from_line(k):
+        arrived(k, 0, 0)
+        to_partner(k)
+        to_sibling(k, 0)
+
+    def from_partner(k):
+        arrived(k, 1, 0)
+        to_sibling(k, 1)
+
+    from_partner(0)
+    from_line(1)
+    arrived(0, 0, 1)
+    arrived(0, 1, 1)
+    compute(0)
+    for k in range(2, depth):
+        from_line(k)
+    from_partner(1)
+    waits = [(k, s) for s in range(2) for k in range(1, depth)]
+    groups = [waits[at : at + TILE // 2] for at in range(0, len(waits), TILE // 2)]
+    forwarded = 1
+    for index, group in enumerate(groups):
+        for k, s in group:
+            if s == 1:
+                while forwarded < k:
+                    forwarded += 1
+                    from_partner(forwarded)
+            arrived(k, s, 1)
+        compute((index + 1) * TILE)
+        if index == 0:
+            while forwarded < depth - 1:
+                forwarded += 1
+                from_partner(forwarded)
+
+    table = jnp.sum(diag[...].T.reshape(n, nocc, 128), axis=1)
     for k in range(depth):
-        slot = slot_of(flip(z, k), other, core)
-        arrived(slot)
-        sent.append(send(slot, core_send.at[depth + k], sibling))
-    compute_group(other, core)
-    for ss in (side, other):
-        for k in range(depth):
-            arrived(slot_of(flip(z, k), ss, 1 - core))
-        compute_group(ss, 1 - core)
-
-    table = jnp.sum(diag[...].T.reshape(n, nocc, 128), axis=1)
-    for w in range(n):
-        slot = slot_of(w // 4, (w // 2) % 2, w % 2)
-        message[w + 1, :, :] = table[slot : slot + 1, :]
-        if w == 0:
-            message[n + 1, :, :] = table[slot : slot + 1, :]
-        if w == n - 1:
-            message[0, :, :] = table[slot : slot + 1, :]
+        for s in range(2):
+            for c in range(2):
+                at = place(k, s, c)
+                w = device_of(flip(z, k), flip(side, s), flip(core, c))
+                message[w + 1, :, :] = table[at : at + 1, :]
+    message[0, :, :] = message[n, :, :]
+    message[n + 1, :, :] = message[1, :, :]
     mail = []
     for k in range(1, n):
         target = (me + k) % n
@@ -180,16 +211,24 @@
         mail.append(copy)
     inbox[pl.ds(me, 1)] = message[pl.ds(me, NEAR)][None]
 
+    def slot_by(w):
+        k, bit = 0, 1
+        while bit < depth:
+            k = k + bit * ((z // bit + w // 4 // bit) % 2)
+            bit *= 2
+        return slot_of(k, (side + w // 2) % 2, (core + w) % 2)
+
+    around = [slot_by((me + n + step) % n) for step in (-1, 0, 1)]
     my_count = counts_ref[me]
     slots = reloc.shape[0]
     chosen = []
     for s in range(slots):
-        w = jnp.clip(source_ref[s], 0, n - 1)
-        slot = slot_of(w // 4, (w // 2) % 2, w % 2)
+        near = lax.rem(jnp.clip(source_ref[s], 0, n - 1) - me + 1 + n, n)
+        near = jnp.minimum(near, NEAR - 1)
         live = s < my_count
+        slot = jnp.where(near == 0, around[0], jnp.where(near == 1, around[1], around[2]))
         value = walkers[slot]
         reloc[s] = jnp.where(live, value, jnp.zeros_like(value))
-        near = jnp.minimum(lax.rem(w - me + 1 + n, n), NEAR - 1)
         chosen.append((near, live))
     store = pltpu.make_async_copy(reloc, reloc_ref, local_sem.at[2])
     store.start()
@@ -224,6 +263,13 @@
     store.wait()
 
 
+def finish(reloc_ref, energy_ref, bias_ref, reloc_out, energy_out, bias_out):
+    reloc_out[...] = reloc_ref[...]
+    bias_out[...] = bias_ref[...]
+    for s in range(energy_ref.shape[0]):
+        energy_out[s] = energy_ref[s]
+
+
 def body(greens, source, counts, cholesky):
     n = lax.axis_size("walk")
     chol_dev, nocc, orbitals = cholesky.shape
@@ -231,7 +277,7 @@
     nchol = chol_dev * n
     assert greens.shape[0] == 1 and nocc == 64 and chol_dev == 32
     depth = n // 4
-    return pl.pallas_call(
+    results = pl.pallas_call(
         functools.partial(kernel, n, nocc, chol_dev, nchol),
         out_shape=(
             jax.ShapeDtypeStruct((slots, nocc, orbitals), jnp.bfloat16),
@@ -252,6 +298,8 @@
         scratch_shapes=[
             pltpu.VMEM((n, nocc, orbitals), jnp.bfloat16),
             pltpu.VMEM((chol_dev * nocc, orbitals), jnp.bfloat16),
+            pltpu.VMEM((orbitals, chol_dev * nocc), jnp.bfloat16),
+            pltpu.VMEM((orbitals, TILE * nocc), jnp.bfloat16),
             pltpu.VMEM((128, n * nocc), jnp.float32),
             pltpu.VMEM((n + 2, 1, 128), jnp.float32),
             pltpu.VMEM((n, NEAR, 1, 128), jnp.float32),
@@ -266,6 +314,13 @@
         ],
         compiler_params=pltpu.CompilerParams(collective_id=0, has_side_effects=True),
     )(source, counts, greens.reshape(nocc, orbitals), cholesky.reshape(chol_dev * nocc, orbitals))
+    places = [pl.BlockSpec(memory_space=m) for m in (pltpu.VMEM, pltpu.SMEM, pltpu.VMEM)]
+    return pl.pallas_call(
+        finish,
+        out_shape=tuple(jax.ShapeDtypeStruct(x.shape, x.dtype) for x in results),
+        in_specs=places,
+        out_specs=tuple(places),
+    )(*results)
 
 
 def solution(mesh):

time: 32.8 us -> 26.5 us (0.81)
  local copies, waits for them, and re-layouts: 3.92 us -> 0 us
  Pallas kernels: 28 us -> 25.7 us
    pallas_call x1, Pallas kernels: 28 us -> 24.1 us  [body(): pl.pallas_call(functools.partial(kernel, n, nocc, chol_dev, nchol), out_s...]
    unnamed x3 -> x0, local copies, waits for them, and re-layouts: 3.92 us -> none
    pallas_call x0 -> x1, Pallas kernels: none -> 1.57 us  [body(): pl.pallas_call(finish, out_shape=tuple((jax.ShapeDtypeStruct(x.shape, x.d...]
where the time goes in v2:
time: 26.5 us; the launch traced here: 26.3 us
  Pallas kernels  25.7 us (97%)
  between operations  0.64 us (2%)
    pallas_call x1, Pallas kernels, body(): pl.pallas_call(functools.partial(kernel, n, nocc, chol_dev, nchol), out_s...  24.1 us
    pallas_call x1, Pallas kernels, body(): pl.pallas_call(finish, out_shape=tuple((jax.ShapeDtypeStruct(x.shape, x.d...  1.57 us

profile of v2, /device:TPU:0, one launch (start us, length us, event | category | flops | bytes accessed | tf_op | source)
XLA Modules:
  0.0 26.3 jit_solution(14104134072419503188)
XLA Ops:
  0.6 24.1 %shard_map.67 = (bf16[2,64,384]{2,1,0:T(8,128)(2,1)}, f32[2]{0:T(128)}, f32[2,512]{1,0:T(2,128)}) custom-call(s32[2]{0:T(128)} %source_ref.1, s32[16]{0:T(128)} %counts_ref.1, bf16[64,384]{1,0:T(8,128)(2,1)} %bitcast.3, bf16[2048,384]{1,0:T(8,128)(2,1)} %bitcast.2), custom_call_target="tpu_custom_call" | custom-call | tf_op jit(solution)/shard_map/pallas_call | solution.py:280
  24.7 1.6 %shard_map.68 = (bf16[2,64,384]{2,1,0:T(8,128)(2,1)}, f32[2]{0:T(128)}, f32[2,512]{1,0:T(2,128)}) custom-call(bf16[2,64,384]{2,1,0:T(8,128)(2,1)} %get-tuple-element.6.reloc_ref, f32[2]{0:T(128)} %get-tuple-element.7.energy_ref, f32[2,512]{1,0:T(2,128)} %get-tuple-element.8.bias_ref), custom_call_target="tpu_custom_call" | custom-call | tf_op jit(solution)/shard_map/pallas_call | solution.py:318
